TPU v7x, 256 devices: a whole 4x4x8 slice. The times are simulated.
256 devices in a mesh: win: 32 (over z_hi, y, core), chan: 8 (over z_lo, x).
Axes of the slice: x: 4, y: 4, z: 8 (z_hi: 4, z_lo: 2; z = z_hi * 2 + z_lo), core: 2. Of those that a mesh axis runs over, the one named last changes fastest.
Arguments:
- traces: bfloat16 [64, 2048, 4096], P('win', 'chan'), may hold values from -120 to 120
- block_pairs: int32 [32, 2], replicated, may hold values from 0 to 15
- valid_count: int32 [1], replicated, may hold values from 8 to 31
Outputs:
- cross_spectra: float32 [32, 8, 2, 128, 128], P('win', 'chan')
Inputs may be any that keep to these rules, and one draw needn't show every extreme that they name: `block_pairs`: entries are channel block numbers; a pair may repeat.
All inputs are finite; a program needn't handle non-finite values.
Results may differ from a plain program's by a relative error of at most 0.0037.
Values may be sent and summed in bfloat16 or wider, within the bound.
No kernel may reach another device: no remote copies, remote signals or barrier semaphores. Data moves between devices by JAX's collectives and lax.ppermute only.
A program may use at most 64 MiB of HBM per device.

v0:
```python
import math
import jax
import jax.numpy as jnp
from jax import lax
from jax.sharding import PartitionSpec as P

BLOCK = 128
NBINS = 256
FREQ_LO = 64
GROUP = 32
EPS = 1e-06


def dft_table(length, first_bin, bins):
    times = jnp.arange(length, dtype=jnp.int32)
    freqs = first_bin + jnp.arange(bins, dtype=jnp.int32)
    phases = times[:, None] * freqs[None, :] % length
    angles = phases.astype(jnp.float32) * (2.0 * math.pi / length)
    factor = 1.0 / math.sqrt(length)
    return (jnp.concatenate([jnp.cos(angles), -jnp.sin(angles)], axis=1) * factor).astype(
        jnp.bfloat16
    )


def block_layout(band_part, block, group):
    windows, channels, _, width = band_part.shape
    shaped = band_part.reshape(windows, channels // block, block, 2, width // group, group)
    rotated = jnp.stack([shaped[:, :, :, 1], -shaped[:, :, :, 0]], axis=3)

    def arrange(values):
        moved = jnp.transpose(values, (1, 4, 2, 0, 3, 5))
        return moved.reshape(channels // block, width // group, block, windows * 2 * group)

    return (arrange(shaped), arrange(rotated))


def pair_products(upper_direct, upper_rotated, lower):
    upper = jnp.concatenate([upper_direct, upper_rotated], axis=2)
    products = jnp.einsum("pgik,pgjk->pgij", upper, lower, preferred_element_type=jnp.float32)
    return products.reshape(products.shape[0], products.shape[1], 2, lower.shape[2], lower.shape[2])


def pair_terms(direct, rotated, chosen):
    return pair_products(direct[chosen[:, 0]], rotated[chosen[:, 0]], direct[chosen[:, 1]])


def on_device(traces, block_pairs, valid_count):
    windows, channels, length = traces.shape
    spectra = jnp.dot(
        traces.reshape(windows * channels, length),
        dft_table(length, FREQ_LO, NBINS),
        preferred_element_type=jnp.float32,
    )
    energy = jnp.sum(spectra * spectra, axis=1, keepdims=True) / NBINS
    whitened = (
        (spectra * lax.rsqrt(energy + EPS))
        .astype(jnp.bfloat16)
        .reshape(windows, channels, 2, NBINS)
    )
    banded = lax.all_to_all(whitened, "chan", split_axis=3, concat_axis=1, tiled=True)
    stack_scale = 1.0 / math.sqrt(windows * lax.axis_size("win") * GROUP)
    slots = block_pairs.shape[0] // lax.axis_size("win")
    first_slot = lax.axis_index("win") * slots
    mine = lax.dynamic_slice_in_dim(block_pairs, first_slot, slots, 0)
    direct, rotated = block_layout(lax.all_gather(banded, "win", axis=0, tiled=True), BLOCK, GROUP)
    stacked = pair_terms(direct, rotated, mine)
    slot_ids = first_slot + jnp.arange(slots, dtype=jnp.int32)
    live = (slot_ids < valid_count[0]).astype(jnp.float32)
    return stacked * stack_scale * live[:, None, None, None, None]


def solution(mesh):
    in_specs = (P("win", "chan", None), P(), P())
    out_specs = P("win", "chan", None, None, None)
    return jax.shard_map(
        on_device, mesh=mesh, in_specs=in_specs, out_specs=out_specs, check_vma=False
    )
```

profile of v0, /device:TPU:43, one launch (start us, length us, event | category | flops | bytes accessed | tf_op | source)
XLA Modules:
  0.0 213.0 jit_solution(3849331905427035691)
XLA Ops:
  6.5 0.0 copy-start
  6.5 16.7 %fusion.10 = (f32[4096,256]{1,0:T(8,128)S(1)}, f32[4096,256]{1,0:T(8,128)S(1)}) fusion(s32[256]{0:T(256)S(1)} %iota_add_fusion), kind=kLoop, calls=%fused_computation.17 | loop fusion | flops 15728640 | bytes 8389632 | tf_op jit(solution)/shard_map/cos | solution.py:20
  23.3 2.5 %multiply_reduce_fusion = (f32[512]{0:T(512)S(1)}, f32[512,512]{1,0:T(8,128)S(1)}) fusion(bf16[512,4096]{1,0:T(8,128)(2,1)S(1)} %bitcast.49, f32[4096,256]{1,0:T(8,128)S(1)} %get-tuple-element.43, f32[4096,256]{1,0:T(8,128)S(1)} %get-tuple-element.42), kind=kOutput, calls=%fused_computation.23 | convolution fusion | flops 2154298880 | bytes 13633536 | tf_op jit(solution)/shard_map/dot_general | solution.py:49
  25.8 0.1 fusion.14
  25.9 0.1 reshape.48
  26.0 0.8 copy.21
  26.8 12.4 %all_to_all.18 = bf16[2,256,2,256]{1,2,0,3:T(2,128)(2,1)S(1)} all-to-all(bf16[2,256,2,256]{1,2,0,3:T(2,128)(2,1)S(1)} %copy.21), channel_id=1, replica_groups=mesh['win'=32,'chan'=8] {'chan'}, dimensions={3} | all-to-all | bytes 1048576 | tf_op jit(solution)/shard_map/all_to_all | solution.py:60
  39.3 0.1 copy.22
  39.3 0.9 copy.28
  40.2 0.0 all-gather.2.cloned.1.call-update
  40.2 0.0 copy-done
  40.2 0.1 constant_dynamic-slice_fusion.2
  40.3 0.5 fusion.19
  45.1 116.9 %all-gather.2.cloned.1.call-done = bf16[64,2048,2,32]{1,3,2,0:T(8,128)(2,1)} async-done(((bf16[2,2048,2,32]{1,3,2,0:T(8,128)(2,1)}), bf16[64,2048,2,32]{1,3,2,0:T(8,128)(2,1)}) %all-gather.2.cloned.1.call-update) | async-done | bytes 16777232 | tf_op jit(solution)/shard_map/all_gather | solution.py:65
  162.0 9.6 %copy.29 = bf16[512,8,16,128]{3,2,1,0:T(8,128)(2,1)S(1)} copy(bf16[512,8,16,128]{3,1,2,0:T(8,128)(2,1)} %bitcast.45) | data formatting | bytes 33554432
  171.7 12.0 %copy.24 = bf16[16,1,128,64,2,32]{2,5,4,3,0,1:T(8,128)(2,1)} copy(bf16[16,1,128,64,2,32]{2,0,5,4,3,1:T(8,128)(2,1)S(1)} %bitcast.40) | data formatting | bytes 33554432 | tf_op jit(solution)/shard_map/transpose | solution.py:31
  183.6 1.7 fusion.18
  185.3 1.7 maximum_bitcast_fusion
  187.0 10.7 %copy.25 = bf16[16,1,128,64,2,32]{2,5,4,3,0,1:T(8,128)(2,1)S(1)} copy(bf16[16,1,128,64,2,32]{2,0,5,4,3,1:T(8,128)(2,1)S(1)} %maximum_bitcast_fusion) | data formatting | bytes 33554432 | tf_op jit(solution)/shard_map/transpose | solution.py:31
  197.7 1.4 constant_dynamic-slice_fusion
  199.0 0.0 copy-start.1
  199.0 1.6 pad_maximum_fusion
  200.6 2.9 %copy.26 = bf16[1,1,256,4096]{3,2,1,0:T(8,128)(2,1)S(1)} copy(bf16[1,1,256,4096]{2,3,0,1:T(8,128)(2,1)} %pad_maximum_fusion) | data formatting | bytes 4194304 | tf_op jit(solution)/shard_map/concatenate | solution.py:38
  203.5 2.6 %fusion.11 = f32[1,1,2,128,128]{4,3,2,1,0:T(8,128)} fusion(bf16[2,128,4096]{2,1,0:T(8,128)(2,1)S(1)} %bitcast.46, bf16[16,1,128,4096]{2,3,0,1:T(8,128)(2,1)} %bitcast.43, s32[]{:T(128)} %bitcast.12, f32[]{:T(128)} %bitcast.16), kind=kOutput, calls=%fused_computation.19 | convolution fusion | flops 268468224 | bytes 3277824 | tf_op jit(solution)/shard_map/pgik,pgjk->pgij/dot_general | solution.py:39
  (6 shorter events, 0.0 us)
Async XLA Ops:
  6.5 33.7 %copy-start = (s32[32,2]{0,1:T(2,128)S(1)}, s32[32,2]{0,1:T(2,128)}, u32[]{:S(2)}) copy-start(s32[32,2]{0,1:T(2,128)} %param.4) | copy-start | bytes 772
  6.5 155.5 %all-gather.2.cloned.1.call-start = ((), (), s32[]{:S(2)}) async-start(), calls=%async_computation.1 | async-start | bytes 17301504 | tf_op jit(solution)/shard_map/all_gather | solution.py:65
  6.5 16.7 %copy-start.2 = (bf16[2,256,4096]{2,1,0:T(8,128)(2,1)S(1)}, bf16[2,256,4096]{2,1,0:T(8,128)(2,1)}, u32[]{:S(2)}) copy-start(bf16[2,256,4096]{2,1,0:T(8,128)(2,1)} %param.3) | copy-start | bytes 12582916
  199.0 7.1 %copy-start.1 = (s32[32,2]{0,1:T(2,128)S(1)}, s32[32,2]{0,1:T(2,128)}, u32[]{:S(2)}) copy-start(s32[32,2]{0,1:T(2,128)} %param.4) | copy-start | bytes 772
Sparse Core Ops, SparseCore 0:
  40.4 121.6 all-gather.1
where the time goes:
time: 213 us
  waiting for transfers between devices  117 us (55%)
  local copies, waits for them, and re-layouts  39 us (18%)
  other arithmetic  21.8 us (10%)
  between operations  17.8 us (8%)
  blocking collectives  12.4 us (6%)
  matrix products  5.11 us (2%)
    all_gather x1, waiting for transfers between devices, on_device(): lax.all_gather(banded, 'win', axis=0, tiled=True)  117 us
    transpose x2, local copies, waits for them, and re-layouts, arrange(): moved = jnp.transpose(values, (1, 4, 2, 0, 3, 5))  22.6 us
    cos x1, other arithmetic, dft_table(): jnp.cos(angles)  16.7 us
    all_to_all x1, blocking collectives, on_device(): lax.all_to_all(whitened, 'chan', split_axis=3, concat_axis=1, tiled=True)  12.4 us
    unnamed x7, local copies, waits for them, and re-layouts  9.66 us
  transfers between devices with their start and end apart: 1, of which 1 were waited for; matrix products, arithmetic and copies ran while one was open for 0% of the time, Pallas kernels for 0%

commit v1 on v0

--- a/solution.py
+++ b/solution.py
@@ -62,7 +62,13 @@
     slots = block_pairs.shape[0] // lax.axis_size("win")
     first_slot = lax.axis_index("win") * slots
     mine = lax.dynamic_slice_in_dim(block_pairs, first_slot, slots, 0)
-    direct, rotated = block_layout(lax.all_gather(banded, "win", axis=0, tiled=True), BLOCK, GROUP)
+    direct, rotated = block_layout(
+        jnp.concatenate(
+            lax.all_to_all(jnp.stack([banded] * lax.axis_size("win")), "win", 0, 0), axis=0
+        ),
+        BLOCK,
+        GROUP,
+    )
     stacked = pair_terms(direct, rotated, mine)
     slot_ids = first_slot + jnp.arange(slots, dtype=jnp.int32)
     live = (slot_ids < valid_count[0]).astype(jnp.float32)

time: 213 us -> 475 us (2.23)
  the two profiles are of different devices: /device:TPU:43 before, /device:TPU:123 now
where the time goes in v1:
time: 475 us
  waiting for transfers between devices  376 us (79%)
  local copies, waits for them, and re-layouts  44.2 us (9%)
  other arithmetic  21.8 us (5%)
  blocking collectives  12.4 us (3%)
  starting transfers between devices  11.2 us (2%)
  matrix products  5.11 us (1%)
    all_to_all x1, waiting for transfers between devices, on_device(): lax.all_to_all(jnp.stack([banded] * lax.axis_size('win')), 'win', 0, 0)  376 us
    transpose x2, local copies, waits for them, and re-layouts, arrange(): moved = jnp.transpose(values, (1, 4, 2, 0, 3, 5))  22.6 us
    cos x1, other arithmetic, dft_table(): jnp.cos(angles)  16.7 us
    all_to_all x1, blocking collectives, on_device(): lax.all_to_all(whitened, 'chan', split_axis=3, concat_axis=1, tiled=True)  12.4 us
    all_to_all x1, starting transfers between devices, on_device(): lax.all_to_all(jnp.stack([banded] * lax.axis_size('win')), 'win', 0, 0)  11.2 us
    unnamed x7, local copies, waits for them, and re-layouts  9.66 us
  transfers between devices with their start and end apart: 1, of which 1 were waited for; matrix products, arithmetic and copies ran while one was open for 0% of the time, Pallas kernels for 0%

profile of v1, /device:TPU:123, one launch (start us, length us, event | category | flops | bytes accessed | tf_op | source)
XLA Modules:
  0.0 474.8 jit_solution(6579077630021551596)
XLA Ops:
  0.0 0.0 copy-start
  0.0 16.7 %fusion.10 = (f32[4096,256]{1,0:T(8,128)S(1)}, f32[4096,256]{1,0:T(8,128)S(1)}) fusion(s32[256]{0:T(256)S(1)} %iota_add_fusion), kind=kLoop, calls=%fused_computation.17 | loop fusion | flops 15728640 | bytes 8389632 | tf_op jit(solution)/shard_map/cos | solution.py:20
  16.7 0.0 copy-done.2
  16.7 2.5 multiply_reduce_fusion
  19.2 0.1 fusion.14
  19.4 0.1 reshape.48
  19.5 0.8 copy.13
  20.3 12.4 %all_to_all.20 = bf16[2,256,2,256]{1,2,0,3:T(2,128)(2,1)S(1)} all-to-all(bf16[2,256,2,256]{1,2,0,3:T(2,128)(2,1)S(1)} %copy.13), channel_id=1, replica_groups=mesh['win'=32,'chan'=8] {'chan'}, dimensions={3} | all-to-all | bytes 1048576 | tf_op jit(solution)/shard_map/all_to_all | solution.py:60
  32.7 0.1 copy.14
  32.9 6.0 %stack.7 = bf16[32,2,2048,2,32]{2,4,3,1,0:T(8,128)(2,1)} broadcast(bf16[2,2048,2,32]{1,3,2,0:T(8,128)(2,1)S(1)} %bitcast.46), dimensions={1,2,3,4} | broadcast | bytes 17301504 | tf_op jit(solution)/shard_map/stack | solution.py:67
  38.8 11.2 %all-to-all-start.1 = ((bf16[32,2,2048,2,32]{2,4,3,1,0:T(8,128)(2,1)}), bf16[32,2,2048,2,32]{2,4,3,1,0:T(8,128)(2,1)}, u32[]{:S(2)}, u32[]{:S(2)}) async-start(bf16[32,2,2048,2,32]{2,4,3,1,0:T(8,128)(2,1)} %stack.7), calls=%async_computation.1 | async-start | bytes 33554432 | tf_op jit(solution)/shard_map/all_to_all | solution.py:67
  50.0 0.1 constant_dynamic-slice_fusion.2
  50.1 0.5 fusion.19
  54.8 375.9 %all-to-all-done.1 = bf16[32,2,2048,2,32]{2,4,3,1,0:T(8,128)(2,1)} async-done(((bf16[32,2,2048,2,32]{2,4,3,1,0:T(8,128)(2,1)}), bf16[32,2,2048,2,32]{2,4,3,1,0:T(8,128)(2,1)}, u32[]{:S(2)}, u32[]{:S(2)}) %all-to-all-start.1) | async-done | bytes 16777248 | tf_op jit(solution)/shard_map/all_to_all | solution.py:67
  430.6 9.6 %copy.21 = bf16[512,8,16,128]{3,2,1,0:T(8,128)(2,1)S(1)} copy(bf16[512,8,16,128]{3,1,2,0:T(8,128)(2,1)} %bitcast.27) | data formatting | bytes 33554432
  440.3 12.0 %copy.16 = bf16[16,1,128,64,2,32]{2,5,4,3,0,1:T(8,128)(2,1)} copy(bf16[16,1,128,64,2,32]{2,0,5,4,3,1:T(8,128)(2,1)S(1)} %bitcast.40) | data formatting | bytes 33554432 | tf_op jit(solution)/shard_map/transpose | solution.py:31
  452.3 1.7 fusion.18
  453.9 1.7 maximum_bitcast_fusion
  455.6 10.7 %copy.17 = bf16[16,1,128,64,2,32]{2,5,4,3,0,1:T(8,128)(2,1)S(1)} copy(bf16[16,1,128,64,2,32]{2,0,5,4,3,1:T(8,128)(2,1)S(1)} %maximum_bitcast_fusion) | data formatting | bytes 33554432 | tf_op jit(solution)/shard_map/transpose | solution.py:31
  466.3 1.4 constant_dynamic-slice_fusion
  467.7 0.0 copy-start.1
  467.7 1.6 pad_maximum_fusion
  469.2 2.9 copy.18
  472.2 2.6 fusion.11
  (6 shorter events, 0.1 us)
Async XLA Ops:
  0.0 50.0 %copy-start = (s32[32,2]{0,1:T(2,128)S(1)}, s32[32,2]{0,1:T(2,128)}, u32[]{:S(2)}) copy-start(s32[32,2]{0,1:T(2,128)} %param.4) | copy-start | bytes 772
  0.0 16.7 %copy-start.2 = (bf16[2,256,4096]{2,1,0:T(8,128)(2,1)S(1)}, bf16[2,256,4096]{2,1,0:T(8,128)(2,1)}, u32[]{:S(2)}) copy-start(bf16[2,256,4096]{2,1,0:T(8,128)(2,1)} %param.3) | copy-start | bytes 12582916
  38.8 391.8 %all-to-all-start.1 = ((bf16[32,2,2048,2,32]{2,4,3,1,0:T(8,128)(2,1)}), bf16[32,2,2048,2,32]{2,4,3,1,0:T(8,128)(2,1)}, u32[]{:S(2)}, u32[]{:S(2)}) async-start(bf16[32,2,2048,2,32]{2,4,3,1,0:T(8,128)(2,1)} %stack.7), calls=%async_computation.1 | async-start | bytes 33554432 | tf_op jit(solution)/shard_map/all_to_all | solution.py:67
  467.7 7.1 %copy-start.1 = (s32[32,2]{0,1:T(2,128)S(1)}, s32[32,2]{0,1:T(2,128)}, u32[]{:S(2)}) copy-start(s32[32,2]{0,1:T(2,128)} %param.4) | copy-start | bytes 772
